TPU v7x, 512 devices: a whole 4x8x8 slice. The times are simulated.
512 devices in a mesh: blk: 64 (over z, y_lo, core), rep: 8 (over y_hi, x).
Axes of the slice: x: 4, y: 8 (y_hi: 2, y_lo: 4; y = y_hi * 4 + y_lo), z: 8, core: 2. Of those that a mesh axis runs over, the one named last changes fastest.
Arguments:
- points: float32 [16, 81920], P(None, ('blk', 'rep')), may hold values from -3 to 3
- vectors: float32 [32, 81920], P(None, ('blk', 'rep')), may hold values from -1.2 to 1.2
- lengthscales: float32 [16], replicated, may hold values from 0.6 to 1.6
Outputs:
- product: float32 [32, 81920], P(None, ('blk', 'rep'))
All inputs are finite; a program needn't handle non-finite values.
Results may differ from a plain program's by a relative error of at most 0.0003.
Values sent between devices are 32-bit elements; how exact they have to be, the bound alone decides.
A program may use at most 64 MiB of HBM per device.

v0:
```python
import jax
import jax.numpy as jnp
from jax import lax
from jax.sharding import PartitionSpec as P


def shifted(value, axis, steps):
    count = lax.axis_size(axis)
    pairs = [(source, (source + steps) % count) for source in range(count)]
    return lax.ppermute(value, axis, pairs)


def matern_tile(col_z, row_z, row_sq):
    col_sq = jnp.sum(col_z * col_z, axis=0)
    cross = lax.dot_general(
        col_z,
        row_z,
        (((0,), (0,)), ((), ())),
        precision=lax.Precision.HIGHEST,
        preferred_element_type=jnp.float32,
    )
    sqdist = jnp.maximum(col_sq[:, None] + row_sq[None, :] - 2.0 * cross, 0.0)
    svalue = jnp.sqrt(5.0 * sqdist)
    return (1.0 + svalue + svalue * svalue / 3.0) * jnp.exp(-svalue)


def rows_times(col_v, kernel):
    return lax.dot(
        col_v, kernel, precision=lax.Precision.HIGHEST, preferred_element_type=jnp.float32
    )


def cols_times(row_v, kernel):
    return lax.dot_general(
        row_v,
        kernel,
        (((1,), (1,)), ((), ())),
        precision=lax.Precision.HIGHEST,
        preferred_element_type=jnp.float32,
    )


def per_device(points, vectors, lengthscales):
    local_z = points / lengthscales[:, None]
    row_z, row_v = (
        lax.all_gather(local_z, "rep", axis=1, tiled=True),
        lax.all_gather(vectors, "rep", axis=1, tiled=True),
    )
    row_sq = jnp.sum(row_z * row_z, axis=0)
    half = lax.axis_size("blk") // 2
    row_acc = rows_times(vectors, matern_tile(local_z, row_z, row_sq))

    def cycle_step(step, carry):
        col_z, col_v, travel, row_total = carry
        col_z, col_v, travel = shifted((col_z, col_v, travel), "blk", 1)
        kernel = matern_tile(col_z, row_z, row_sq)
        return (
            col_z,
            col_v,
            travel + cols_times(row_v, kernel),
            row_total + rows_times(col_v, kernel),
        )

    start = (local_z, vectors, jnp.zeros_like(vectors), row_acc)
    col_z, col_v, travel, row_acc = lax.fori_loop(1, half, cycle_step, start)
    col_z, col_v = shifted((col_z, col_v), "blk", 1)
    returned = shifted(travel, "blk", 1 - half)
    row_acc = row_acc + rows_times(col_v, matern_tile(col_z, row_z, row_sq))
    return lax.psum_scatter(row_acc, "rep", scatter_dimension=1, tiled=True) + returned


def solution(mesh):
    return jax.shard_map(
        per_device,
        mesh=mesh,
        in_specs=(P(None, ("blk", "rep")), P(None, ("blk", "rep")), P()),
        out_specs=P(None, ("blk", "rep")),
        check_vma=False,
    )
```

profile of v0, /device:TPU:2, one launch (start us, length us, event | category | flops | bytes accessed | tf_op | source)
XLA Modules:
  0.0 664.6 jit_solution(17798006925289154229)
XLA Ops:
  8.1 44.3 %all-gather = f32[8,160,16]{1,2,0:T(8,128)S(1)} all-gather(f32[1,160,16]{1,2,0:T(8,128)S(1)} %bitcast.59), channel_id=1, replica_groups=mesh['blk'=64,'rep'=8] {'rep'}, dimensions={0}, use_global_device_ids=true | all-gather | bytes 92160 | tf_op jit(solution)/shard_map/all_gather | solution.py:46
  54.4 44.0 %all-gather.1 = f32[8,160,32]{1,2,0:T(8,128)S(1)} all-gather(f32[1,160,32]{1,2,0:T(8,128)S(1)} %bitcast.57), channel_id=1, replica_groups=mesh['blk'=64,'rep'=8] {'rep'}, dimensions={0}, use_global_device_ids=true | all-gather | bytes 184320 | tf_op jit(solution)/shard_map/all_gather | solution.py:47
  98.7 449.9 %while.17 = (s32[]{:T(128)}, f32[16,160]{1,0:T(8,128)S(1)}, f32[32,160]{1,0:T(8,128)S(1)}, f32[32,160]{1,0:T(8,128)S(1)}, f32[32,1280]{1,0:T(8,128)S(1)}, /*inde...) while((s32[]{:T(128)}, f32[16,160]{1,0:T(8,128)S(1)}, ...), condition=%wide.region_4.0_spmd.clone, body=%wide.region_2.0_spmd.clone.sunk | while | flops 198916960 | bytes 3426791 | solution.py:65
  109.0 3.6 collective-permute-done.1
  119.8 3.2 collective-permute-done
  124.3 2.8 collective-permute-done.1
  134.3 3.2 collective-permute-done
  148.8 3.2 collective-permute-done
  153.3 2.8 collective-permute-done.1
  163.3 3.2 collective-permute-done
  177.8 3.2 collective-permute-done
  182.2 2.8 collective-permute-done.1
  192.3 3.2 collective-permute-done
  206.8 3.2 collective-permute-done
  221.2 3.2 collective-permute-done
  225.7 2.8 collective-permute-done.1
  235.7 3.2 collective-permute-done
  250.2 3.2 collective-permute-done
  254.7 2.8 collective-permute-done.1
  264.7 3.2 collective-permute-done
  279.2 3.2 collective-permute-done
  293.7 3.2 collective-permute-done
  298.1 2.8 collective-permute-done.1
  308.2 3.2 collective-permute-done
  322.7 3.2 collective-permute-done
  327.1 2.8 collective-permute-done.1
  337.1 3.2 collective-permute-done
  351.6 3.2 collective-permute-done
  366.1 3.2 collective-permute-done
  370.6 2.8 collective-permute-done.1
  380.6 3.2 collective-permute-done
  395.1 3.2 collective-permute-done
  399.5 2.8 collective-permute-done.1
  409.6 3.2 collective-permute-done
  424.1 3.2 collective-permute-done
  438.6 3.2 collective-permute-done
  443.0 2.8 collective-permute-done.1
  453.0 3.2 collective-permute-done
  467.5 3.2 collective-permute-done
  472.0 2.8 collective-permute-done.1
  482.0 3.2 collective-permute-done
  496.5 3.2 collective-permute-done
  511.0 3.2 collective-permute-done
  525.5 3.2 collective-permute-done
  540.0 3.2 collective-permute-done
  552.5 5.1 collective-permute-done.4
  562.3 4.2 collective-permute-start.5
  566.5 89.7 %reduce-scatter.4.cloned.1.call-done = f32[160,32]{1,0:T(8,128)} async-done(((f32[1280,32]{1,0:T(8,128)}), f32[160,32]{1,0:T(8,128)}) %reduce-scatter.4.cloned.1.call-update) | async-done | bytes 20496
  (387 shorter events, 332.0 us)
Async XLA Ops:
  6.5 649.6 %reduce-scatter.4.cloned.1.call-start = ((), (), s32[]{:S(2)}) async-start(), calls=%async_computation.1 | async-start | bytes 737280
  100.7 12.5 %collective-permute-start.2 = (f32[32,160]{1,0:T(8,128)S(1)}, f32[32,160]{1,0:T(8,128)S(1)}, u32[]{:S(2)}, u32[]{:S(2)}) collective-permute-start(f32[32,160]{1,0:T(8,128)S(1)} %broadcast_select_fusion.2), channel_id=1, source_target_pairs={{0,8},{8,16},{16,24},{24,32},{32,40},{40,48},{48,56},{56,64},{64,7... | collective-permute-start | bytes 61448 | tf_op jit(solution)/shard_map/while/body/eval_jaxpr/ppermute | solution.py:10
  103.4 9.1 %collective-permute-start.1 = (f32[32,160]{1,0:T(8,128)S(1)}, f32[32,160]{1,0:T(8,128)S(1)}, u32[]{:S(2)}, u32[]{:S(2)}) collective-permute-start(f32[32,160]{1,0:T(8,128)S(1)} %get-tuple-element.160), channel_id=1, source_target_pairs={{0,8},{8,16},{16,24},{24,32},{32,40},{40,48},{48,56},{56,64},{64,7... | collective-permute-start | bytes 61448 | tf_op jit(solution)/shard_map/while/body/eval_jaxpr/ppermute | solution.py:10
  116.0 11.7 %collective-permute-start.2 = (f32[32,160]{1,0:T(8,128)S(1)}, f32[32,160]{1,0:T(8,128)S(1)}, u32[]{:S(2)}, u32[]{:S(2)}) collective-permute-start(f32[32,160]{1,0:T(8,128)S(1)} %broadcast_select_fusion.2), channel_id=1, source_target_pairs={{0,8},{8,16},{16,24},{24,32},{32,40},{40,48},{48,56},{56,64},{64,7... | collective-permute-start | bytes 61448 | tf_op jit(solution)/shard_map/while/body/eval_jaxpr/ppermute | solution.py:10
  117.9 9.1 %collective-permute-start.1 = (f32[32,160]{1,0:T(8,128)S(1)}, f32[32,160]{1,0:T(8,128)S(1)}, u32[]{:S(2)}, u32[]{:S(2)}) collective-permute-start(f32[32,160]{1,0:T(8,128)S(1)} %get-tuple-element.160), channel_id=1, source_target_pairs={{0,8},{8,16},{16,24},{24,32},{32,40},{40,48},{48,56},{56,64},{64,7... | collective-permute-start | bytes 61448 | tf_op jit(solution)/shard_map/while/body/eval_jaxpr/ppermute | solution.py:10
  130.5 11.7 %collective-permute-start.2 = (f32[32,160]{1,0:T(8,128)S(1)}, f32[32,160]{1,0:T(8,128)S(1)}, u32[]{:S(2)}, u32[]{:S(2)}) collective-permute-start(f32[32,160]{1,0:T(8,128)S(1)} %broadcast_select_fusion.2), channel_id=1, source_target_pairs={{0,8},{8,16},{16,24},{24,32},{32,40},{40,48},{48,56},{56,64},{64,7... | collective-permute-start | bytes 61448 | tf_op jit(solution)/shard_map/while/body/eval_jaxpr/ppermute | solution.py:10
  132.4 9.1 %collective-permute-start.1 = (f32[32,160]{1,0:T(8,128)S(1)}, f32[32,160]{1,0:T(8,128)S(1)}, u32[]{:S(2)}, u32[]{:S(2)}) collective-permute-start(f32[32,160]{1,0:T(8,128)S(1)} %get-tuple-element.160), channel_id=1, source_target_pairs={{0,8},{8,16},{16,24},{24,32},{32,40},{40,48},{48,56},{56,64},{64,7... | collective-permute-start | bytes 61448 | tf_op jit(solution)/shard_map/while/body/eval_jaxpr/ppermute | solution.py:10
  145.0 11.7 %collective-permute-start.2 = (f32[32,160]{1,0:T(8,128)S(1)}, f32[32,160]{1,0:T(8,128)S(1)}, u32[]{:S(2)}, u32[]{:S(2)}) collective-permute-start(f32[32,160]{1,0:T(8,128)S(1)} %broadcast_select_fusion.2), channel_id=1, source_target_pairs={{0,8},{8,16},{16,24},{24,32},{32,40},{40,48},{48,56},{56,64},{64,7... | collective-permute-start | bytes 61448 | tf_op jit(solution)/shard_map/while/body/eval_jaxpr/ppermute | solution.py:10
  159.4 11.7 %collective-permute-start.2 = (f32[32,160]{1,0:T(8,128)S(1)}, f32[32,160]{1,0:T(8,128)S(1)}, u32[]{:S(2)}, u32[]{:S(2)}) collective-permute-start(f32[32,160]{1,0:T(8,128)S(1)} %broadcast_select_fusion.2), channel_id=1, source_target_pairs={{0,8},{8,16},{16,24},{24,32},{32,40},{40,48},{48,56},{56,64},{64,7... | collective-permute-start | bytes 61448 | tf_op jit(solution)/shard_map/while/body/eval_jaxpr/ppermute | solution.py:10
  173.9 11.7 %collective-permute-start.2 = (f32[32,160]{1,0:T(8,128)S(1)}, f32[32,160]{1,0:T(8,128)S(1)}, u32[]{:S(2)}, u32[]{:S(2)}) collective-permute-start(f32[32,160]{1,0:T(8,128)S(1)} %broadcast_select_fusion.2), channel_id=1, source_target_pairs={{0,8},{8,16},{16,24},{24,32},{32,40},{40,48},{48,56},{56,64},{64,7... | collective-permute-start | bytes 61448 | tf_op jit(solution)/shard_map/while/body/eval_jaxpr/ppermute | solution.py:10
  175.9 9.1 %collective-permute-start.1 = (f32[32,160]{1,0:T(8,128)S(1)}, f32[32,160]{1,0:T(8,128)S(1)}, u32[]{:S(2)}, u32[]{:S(2)}) collective-permute-start(f32[32,160]{1,0:T(8,128)S(1)} %get-tuple-element.160), channel_id=1, source_target_pairs={{0,8},{8,16},{16,24},{24,32},{32,40},{40,48},{48,56},{56,64},{64,7... | collective-permute-start | bytes 61448 | tf_op jit(solution)/shard_map/while/body/eval_jaxpr/ppermute | solution.py:10
  188.4 11.7 %collective-permute-start.2 = (f32[32,160]{1,0:T(8,128)S(1)}, f32[32,160]{1,0:T(8,128)S(1)}, u32[]{:S(2)}, u32[]{:S(2)}) collective-permute-start(f32[32,160]{1,0:T(8,128)S(1)} %broadcast_select_fusion.2), channel_id=1, source_target_pairs={{0,8},{8,16},{16,24},{24,32},{32,40},{40,48},{48,56},{56,64},{64,7... | collective-permute-start | bytes 61448 | tf_op jit(solution)/shard_map/while/body/eval_jaxpr/ppermute | solution.py:10
  190.3 9.1 %collective-permute-start.1 = (f32[32,160]{1,0:T(8,128)S(1)}, f32[32,160]{1,0:T(8,128)S(1)}, u32[]{:S(2)}, u32[]{:S(2)}) collective-permute-start(f32[32,160]{1,0:T(8,128)S(1)} %get-tuple-element.160), channel_id=1, source_target_pairs={{0,8},{8,16},{16,24},{24,32},{32,40},{40,48},{48,56},{56,64},{64,7... | collective-permute-start | bytes 61448 | tf_op jit(solution)/shard_map/while/body/eval_jaxpr/ppermute | solution.py:10
  202.9 11.7 %collective-permute-start.2 = (f32[32,160]{1,0:T(8,128)S(1)}, f32[32,160]{1,0:T(8,128)S(1)}, u32[]{:S(2)}, u32[]{:S(2)}) collective-permute-start(f32[32,160]{1,0:T(8,128)S(1)} %broadcast_select_fusion.2), channel_id=1, source_target_pairs={{0,8},{8,16},{16,24},{24,32},{32,40},{40,48},{48,56},{56,64},{64,7... | collective-permute-start | bytes 61448 | tf_op jit(solution)/shard_map/while/body/eval_jaxpr/ppermute | solution.py:10
  204.8 9.1 %collective-permute-start.1 = (f32[32,160]{1,0:T(8,128)S(1)}, f32[32,160]{1,0:T(8,128)S(1)}, u32[]{:S(2)}, u32[]{:S(2)}) collective-permute-start(f32[32,160]{1,0:T(8,128)S(1)} %get-tuple-element.160), channel_id=1, source_target_pairs={{0,8},{8,16},{16,24},{24,32},{32,40},{40,48},{48,56},{56,64},{64,7... | collective-permute-start | bytes 61448 | tf_op jit(solution)/shard_map/while/body/eval_jaxpr/ppermute | solution.py:10
  217.4 11.7 %collective-permute-start.2 = (f32[32,160]{1,0:T(8,128)S(1)}, f32[32,160]{1,0:T(8,128)S(1)}, u32[]{:S(2)}, u32[]{:S(2)}) collective-permute-start(f32[32,160]{1,0:T(8,128)S(1)} %broadcast_select_fusion.2), channel_id=1, source_target_pairs={{0,8},{8,16},{16,24},{24,32},{32,40},{40,48},{48,56},{56,64},{64,7... | collective-permute-start | bytes 61448 | tf_op jit(solution)/shard_map/while/body/eval_jaxpr/ppermute | solution.py:10
  219.3 9.1 %collective-permute-start.1 = (f32[32,160]{1,0:T(8,128)S(1)}, f32[32,160]{1,0:T(8,128)S(1)}, u32[]{:S(2)}, u32[]{:S(2)}) collective-permute-start(f32[32,160]{1,0:T(8,128)S(1)} %get-tuple-element.160), channel_id=1, source_target_pairs={{0,8},{8,16},{16,24},{24,32},{32,40},{40,48},{48,56},{56,64},{64,7... | collective-permute-start | bytes 61448 | tf_op jit(solution)/shard_map/while/body/eval_jaxpr/ppermute | solution.py:10
  231.9 11.7 %collective-permute-start.2 = (f32[32,160]{1,0:T(8,128)S(1)}, f32[32,160]{1,0:T(8,128)S(1)}, u32[]{:S(2)}, u32[]{:S(2)}) collective-permute-start(f32[32,160]{1,0:T(8,128)S(1)} %broadcast_select_fusion.2), channel_id=1, source_target_pairs={{0,8},{8,16},{16,24},{24,32},{32,40},{40,48},{48,56},{56,64},{64,7... | collective-permute-start | bytes 61448 | tf_op jit(solution)/shard_map/while/body/eval_jaxpr/ppermute | solution.py:10
  246.4 11.7 %collective-permute-start.2 = (f32[32,160]{1,0:T(8,128)S(1)}, f32[32,160]{1,0:T(8,128)S(1)}, u32[]{:S(2)}, u32[]{:S(2)}) collective-permute-start(f32[32,160]{1,0:T(8,128)S(1)} %broadcast_select_fusion.2), channel_id=1, source_target_pairs={{0,8},{8,16},{16,24},{24,32},{32,40},{40,48},{48,56},{56,64},{64,7... | collective-permute-start | bytes 61448 | tf_op jit(solution)/shard_map/while/body/eval_jaxpr/ppermute | solution.py:10
  248.3 9.1 %collective-permute-start.1 = (f32[32,160]{1,0:T(8,128)S(1)}, f32[32,160]{1,0:T(8,128)S(1)}, u32[]{:S(2)}, u32[]{:S(2)}) collective-permute-start(f32[32,160]{1,0:T(8,128)S(1)} %get-tuple-element.160), channel_id=1, source_target_pairs={{0,8},{8,16},{16,24},{24,32},{32,40},{40,48},{48,56},{56,64},{64,7... | collective-permute-start | bytes 61448 | tf_op jit(solution)/shard_map/while/body/eval_jaxpr/ppermute | solution.py:10
  260.9 11.7 %collective-permute-start.2 = (f32[32,160]{1,0:T(8,128)S(1)}, f32[32,160]{1,0:T(8,128)S(1)}, u32[]{:S(2)}, u32[]{:S(2)}) collective-permute-start(f32[32,160]{1,0:T(8,128)S(1)} %broadcast_select_fusion.2), channel_id=1, source_target_pairs={{0,8},{8,16},{16,24},{24,32},{32,40},{40,48},{48,56},{56,64},{64,7... | collective-permute-start | bytes 61448 | tf_op jit(solution)/shard_map/while/body/eval_jaxpr/ppermute | solution.py:10
  262.8 9.1 %collective-permute-start.1 = (f32[32,160]{1,0:T(8,128)S(1)}, f32[32,160]{1,0:T(8,128)S(1)}, u32[]{:S(2)}, u32[]{:S(2)}) collective-permute-start(f32[32,160]{1,0:T(8,128)S(1)} %get-tuple-element.160), channel_id=1, source_target_pairs={{0,8},{8,16},{16,24},{24,32},{32,40},{40,48},{48,56},{56,64},{64,7... | collective-permute-start | bytes 61448 | tf_op jit(solution)/shard_map/while/body/eval_jaxpr/ppermute | solution.py:10
  275.3 11.7 %collective-permute-start.2 = (f32[32,160]{1,0:T(8,128)S(1)}, f32[32,160]{1,0:T(8,128)S(1)}, u32[]{:S(2)}, u32[]{:S(2)}) collective-permute-start(f32[32,160]{1,0:T(8,128)S(1)} %broadcast_select_fusion.2), channel_id=1, source_target_pairs={{0,8},{8,16},{16,24},{24,32},{32,40},{40,48},{48,56},{56,64},{64,7... | collective-permute-start | bytes 61448 | tf_op jit(solution)/shard_map/while/body/eval_jaxpr/ppermute | solution.py:10
  289.8 11.7 %collective-permute-start.2 = (f32[32,160]{1,0:T(8,128)S(1)}, f32[32,160]{1,0:T(8,128)S(1)}, u32[]{:S(2)}, u32[]{:S(2)}) collective-permute-start(f32[32,160]{1,0:T(8,128)S(1)} %broadcast_select_fusion.2), channel_id=1, source_target_pairs={{0,8},{8,16},{16,24},{24,32},{32,40},{40,48},{48,56},{56,64},{64,7... | collective-permute-start | bytes 61448 | tf_op jit(solution)/shard_map/while/body/eval_jaxpr/ppermute | solution.py:10
  291.8 9.1 %collective-permute-start.1 = (f32[32,160]{1,0:T(8,128)S(1)}, f32[32,160]{1,0:T(8,128)S(1)}, u32[]{:S(2)}, u32[]{:S(2)}) collective-permute-start(f32[32,160]{1,0:T(8,128)S(1)} %get-tuple-element.160), channel_id=1, source_target_pairs={{0,8},{8,16},{16,24},{24,32},{32,40},{40,48},{48,56},{56,64},{64,7... | collective-permute-start | bytes 61448 | tf_op jit(solution)/shard_map/while/body/eval_jaxpr/ppermute | solution.py:10
  304.3 11.7 %collective-permute-start.2 = (f32[32,160]{1,0:T(8,128)S(1)}, f32[32,160]{1,0:T(8,128)S(1)}, u32[]{:S(2)}, u32[]{:S(2)}) collective-permute-start(f32[32,160]{1,0:T(8,128)S(1)} %broadcast_select_fusion.2), channel_id=1, source_target_pairs={{0,8},{8,16},{16,24},{24,32},{32,40},{40,48},{48,56},{56,64},{64,7... | collective-permute-start | bytes 61448 | tf_op jit(solution)/shard_map/while/body/eval_jaxpr/ppermute | solution.py:10
  306.2 9.1 %collective-permute-start.1 = (f32[32,160]{1,0:T(8,128)S(1)}, f32[32,160]{1,0:T(8,128)S(1)}, u32[]{:S(2)}, u32[]{:S(2)}) collective-permute-start(f32[32,160]{1,0:T(8,128)S(1)} %get-tuple-element.160), channel_id=1, source_target_pairs={{0,8},{8,16},{16,24},{24,32},{32,40},{40,48},{48,56},{56,64},{64,7... | collective-permute-start | bytes 61448 | tf_op jit(solution)/shard_map/while/body/eval_jaxpr/ppermute | solution.py:10
  318.8 11.7 %collective-permute-start.2 = (f32[32,160]{1,0:T(8,128)S(1)}, f32[32,160]{1,0:T(8,128)S(1)}, u32[]{:S(2)}, u32[]{:S(2)}) collective-permute-start(f32[32,160]{1,0:T(8,128)S(1)} %broadcast_select_fusion.2), channel_id=1, source_target_pairs={{0,8},{8,16},{16,24},{24,32},{32,40},{40,48},{48,56},{56,64},{64,7... | collective-permute-start | bytes 61448 | tf_op jit(solution)/shard_map/while/body/eval_jaxpr/ppermute | solution.py:10
  320.7 9.1 %collective-permute-start.1 = (f32[32,160]{1,0:T(8,128)S(1)}, f32[32,160]{1,0:T(8,128)S(1)}, u32[]{:S(2)}, u32[]{:S(2)}) collective-permute-start(f32[32,160]{1,0:T(8,128)S(1)} %get-tuple-element.160), channel_id=1, source_target_pairs={{0,8},{8,16},{16,24},{24,32},{32,40},{40,48},{48,56},{56,64},{64,7... | collective-permute-start | bytes 61448 | tf_op jit(solution)/shard_map/while/body/eval_jaxpr/ppermute | solution.py:10
  333.3 11.7 %collective-permute-start.2 = (f32[32,160]{1,0:T(8,128)S(1)}, f32[32,160]{1,0:T(8,128)S(1)}, u32[]{:S(2)}, u32[]{:S(2)}) collective-permute-start(f32[32,160]{1,0:T(8,128)S(1)} %broadcast_select_fusion.2), channel_id=1, source_target_pairs={{0,8},{8,16},{16,24},{24,32},{32,40},{40,48},{48,56},{56,64},{64,7... | collective-permute-start | bytes 61448 | tf_op jit(solution)/shard_map/while/body/eval_jaxpr/ppermute | solution.py:10
  347.8 11.7 %collective-permute-start.2 = (f32[32,160]{1,0:T(8,128)S(1)}, f32[32,160]{1,0:T(8,128)S(1)}, u32[]{:S(2)}, u32[]{:S(2)}) collective-permute-start(f32[32,160]{1,0:T(8,128)S(1)} %broadcast_select_fusion.2), channel_id=1, source_target_pairs={{0,8},{8,16},{16,24},{24,32},{32,40},{40,48},{48,56},{56,64},{64,7... | collective-permute-start | bytes 61448 | tf_op jit(solution)/shard_map/while/body/eval_jaxpr/ppermute | solution.py:10
  362.3 11.7 %collective-permute-start.2 = (f32[32,160]{1,0:T(8,128)S(1)}, f32[32,160]{1,0:T(8,128)S(1)}, u32[]{:S(2)}, u32[]{:S(2)}) collective-permute-start(f32[32,160]{1,0:T(8,128)S(1)} %broadcast_select_fusion.2), channel_id=1, source_target_pairs={{0,8},{8,16},{16,24},{24,32},{32,40},{40,48},{48,56},{56,64},{64,7... | collective-permute-start | bytes 61448 | tf_op jit(solution)/shard_map/while/body/eval_jaxpr/ppermute | solution.py:10
  364.2 9.1 %collective-permute-start.1 = (f32[32,160]{1,0:T(8,128)S(1)}, f32[32,160]{1,0:T(8,128)S(1)}, u32[]{:S(2)}, u32[]{:S(2)}) collective-permute-start(f32[32,160]{1,0:T(8,128)S(1)} %get-tuple-element.160), channel_id=1, source_target_pairs={{0,8},{8,16},{16,24},{24,32},{32,40},{40,48},{48,56},{56,64},{64,7... | collective-permute-start | bytes 61448 | tf_op jit(solution)/shard_map/while/body/eval_jaxpr/ppermute | solution.py:10
  376.8 11.7 %collective-permute-start.2 = (f32[32,160]{1,0:T(8,128)S(1)}, f32[32,160]{1,0:T(8,128)S(1)}, u32[]{:S(2)}, u32[]{:S(2)}) collective-permute-start(f32[32,160]{1,0:T(8,128)S(1)} %broadcast_select_fusion.2), channel_id=1, source_target_pairs={{0,8},{8,16},{16,24},{24,32},{32,40},{40,48},{48,56},{56,64},{64,7... | collective-permute-start | bytes 61448 | tf_op jit(solution)/shard_map/while/body/eval_jaxpr/ppermute | solution.py:10
  378.7 9.1 %collective-permute-start.1 = (f32[32,160]{1,0:T(8,128)S(1)}, f32[32,160]{1,0:T(8,128)S(1)}, u32[]{:S(2)}, u32[]{:S(2)}) collective-permute-start(f32[32,160]{1,0:T(8,128)S(1)} %get-tuple-element.160), channel_id=1, source_target_pairs={{0,8},{8,16},{16,24},{24,32},{32,40},{40,48},{48,56},{56,64},{64,7... | collective-permute-start | bytes 61448 | tf_op jit(solution)/shard_map/while/body/eval_jaxpr/ppermute | solution.py:10
  391.2 11.7 %collective-permute-start.2 = (f32[32,160]{1,0:T(8,128)S(1)}, f32[32,160]{1,0:T(8,128)S(1)}, u32[]{:S(2)}, u32[]{:S(2)}) collective-permute-start(f32[32,160]{1,0:T(8,128)S(1)} %broadcast_select_fusion.2), channel_id=1, source_target_pairs={{0,8},{8,16},{16,24},{24,32},{32,40},{40,48},{48,56},{56,64},{64,7... | collective-permute-start | bytes 61448 | tf_op jit(solution)/shard_map/while/body/eval_jaxpr/ppermute | solution.py:10
  405.7 11.7 %collective-permute-start.2 = (f32[32,160]{1,0:T(8,128)S(1)}, f32[32,160]{1,0:T(8,128)S(1)}, u32[]{:S(2)}, u32[]{:S(2)}) collective-permute-start(f32[32,160]{1,0:T(8,128)S(1)} %broadcast_select_fusion.2), channel_id=1, source_target_pairs={{0,8},{8,16},{16,24},{24,32},{32,40},{40,48},{48,56},{56,64},{64,7... | collective-permute-start | bytes 61448 | tf_op jit(solution)/shard_map/while/body/eval_jaxpr/ppermute | solution.py:10
  420.2 11.7 %collective-permute-start.2 = (f32[32,160]{1,0:T(8,128)S(1)}, f32[32,160]{1,0:T(8,128)S(1)}, u32[]{:S(2)}, u32[]{:S(2)}) collective-permute-start(f32[32,160]{1,0:T(8,128)S(1)} %broadcast_select_fusion.2), channel_id=1, source_target_pairs={{0,8},{8,16},{16,24},{24,32},{32,40},{40,48},{48,56},{56,64},{64,7... | collective-permute-start | bytes 61448 | tf_op jit(solution)/shard_map/while/body/eval_jaxpr/ppermute | solution.py:10
  434.7 11.7 %collective-permute-start.2 = (f32[32,160]{1,0:T(8,128)S(1)}, f32[32,160]{1,0:T(8,128)S(1)}, u32[]{:S(2)}, u32[]{:S(2)}) collective-permute-start(f32[32,160]{1,0:T(8,128)S(1)} %broadcast_select_fusion.2), channel_id=1, source_target_pairs={{0,8},{8,16},{16,24},{24,32},{32,40},{40,48},{48,56},{56,64},{64,7... | collective-permute-start | bytes 61448 | tf_op jit(solution)/shard_map/while/body/eval_jaxpr/ppermute | solution.py:10
  449.2 11.7 %collective-permute-start.2 = (f32[32,160]{1,0:T(8,128)S(1)}, f32[32,160]{1,0:T(8,128)S(1)}, u32[]{:S(2)}, u32[]{:S(2)}) collective-permute-start(f32[32,160]{1,0:T(8,128)S(1)} %broadcast_select_fusion.2), channel_id=1, source_target_pairs={{0,8},{8,16},{16,24},{24,32},{32,40},{40,48},{48,56},{56,64},{64,7... | collective-permute-start | bytes 61448 | tf_op jit(solution)/shard_map/while/body/eval_jaxpr/ppermute | solution.py:10
  463.7 11.7 %collective-permute-start.2 = (f32[32,160]{1,0:T(8,128)S(1)}, f32[32,160]{1,0:T(8,128)S(1)}, u32[]{:S(2)}, u32[]{:S(2)}) collective-permute-start(f32[32,160]{1,0:T(8,128)S(1)} %broadcast_select_fusion.2), channel_id=1, source_target_pairs={{0,8},{8,16},{16,24},{24,32},{32,40},{40,48},{48,56},{56,64},{64,7... | collective-permute-start | bytes 61448 | tf_op jit(solution)/shard_map/while/body/eval_jaxpr/ppermute | solution.py:10
  478.2 11.7 %collective-permute-start.2 = (f32[32,160]{1,0:T(8,128)S(1)}, f32[32,160]{1,0:T(8,128)S(1)}, u32[]{:S(2)}, u32[]{:S(2)}) collective-permute-start(f32[32,160]{1,0:T(8,128)S(1)} %broadcast_select_fusion.2), channel_id=1, source_target_pairs={{0,8},{8,16},{16,24},{24,32},{32,40},{40,48},{48,56},{56,64},{64,7... | collective-permute-start | bytes 61448 | tf_op jit(solution)/shard_map/while/body/eval_jaxpr/ppermute | solution.py:10
  492.7 11.7 %collective-permute-start.2 = (f32[32,160]{1,0:T(8,128)S(1)}, f32[32,160]{1,0:T(8,128)S(1)}, u32[]{:S(2)}, u32[]{:S(2)}) collective-permute-start(f32[32,160]{1,0:T(8,128)S(1)} %broadcast_select_fusion.2), channel_id=1, source_target_pairs={{0,8},{8,16},{16,24},{24,32},{32,40},{40,48},{48,56},{56,64},{64,7... | collective-permute-start | bytes 61448 | tf_op jit(solution)/shard_map/while/body/eval_jaxpr/ppermute | solution.py:10
  507.1 11.7 %collective-permute-start.2 = (f32[32,160]{1,0:T(8,128)S(1)}, f32[32,160]{1,0:T(8,128)S(1)}, u32[]{:S(2)}, u32[]{:S(2)}) collective-permute-start(f32[32,160]{1,0:T(8,128)S(1)} %broadcast_select_fusion.2), channel_id=1, source_target_pairs={{0,8},{8,16},{16,24},{24,32},{32,40},{40,48},{48,56},{56,64},{64,7... | collective-permute-start | bytes 61448 | tf_op jit(solution)/shard_map/while/body/eval_jaxpr/ppermute | solution.py:10
  521.6 11.7 %collective-permute-start.2 = (f32[32,160]{1,0:T(8,128)S(1)}, f32[32,160]{1,0:T(8,128)S(1)}, u32[]{:S(2)}, u32[]{:S(2)}) collective-permute-start(f32[32,160]{1,0:T(8,128)S(1)} %broadcast_select_fusion.2), channel_id=1, source_target_pairs={{0,8},{8,16},{16,24},{24,32},{32,40},{40,48},{48,56},{56,64},{64,7... | collective-permute-start | bytes 61448 | tf_op jit(solution)/shard_map/while/body/eval_jaxpr/ppermute | solution.py:10
  536.1 11.7 %collective-permute-start.2 = (f32[32,160]{1,0:T(8,128)S(1)}, f32[32,160]{1,0:T(8,128)S(1)}, u32[]{:S(2)}, u32[]{:S(2)}) collective-permute-start(f32[32,160]{1,0:T(8,128)S(1)} %broadcast_select_fusion.2), channel_id=1, source_target_pairs={{0,8},{8,16},{16,24},{24,32},{32,40},{40,48},{48,56},{56,64},{64,7... | collective-permute-start | bytes 61448 | tf_op jit(solution)/shard_map/while/body/eval_jaxpr/ppermute | solution.py:10
  550.6 9.4 %collective-permute-start.3 = (f32[32,160]{1,0:T(8,128)S(1)}, f32[32,160]{1,0:T(8,128)S(1)}, u32[]{:S(2)}, u32[]{:S(2)}) collective-permute-start(f32[32,160]{1,0:T(8,128)S(1)} %get-tuple-element.51), channel_id=1, source_target_pairs={{0,8},{8,16},{16,24},{24,32},{32,40},{40,48},{48,56},{56,64},{64,7... | collective-permute-start | bytes 61448 | tf_op jit(solution)/shard_map/ppermute | solution.py:10
  562.3 94.8 %collective-permute-start.5 = (f32[32,160]{1,0:T(8,128)S(1)}, f32[32,160]{1,0:T(8,128)S(1)}, u32[]{:S(2)}, u32[]{:S(2)}) collective-permute-start(f32[32,160]{1,0:T(8,128)S(1)} %get-tuple-element.53), channel_id=1, source_target_pairs={{0,264},{8,272},{16,280},{24,288},{32,296},{40,304},{48,312},{56,3... | collective-permute-start | bytes 61448 | tf_op jit(solution)/shard_map/ppermute | solution.py:10
  (51 other events, 443.7 us)
Sparse Core Ops, SparseCore 0:
  562.4 93.7 reduce-scatter.3
where the time goes:
time: 668 us; the launch traced here: 665 us
  waiting for transfers between devices  280 us (42%)
  starting transfers between devices  187 us (28%)
  blocking collectives  88.4 us (13%)
  matrix products  86.7 us (13%)
  between operations  13.5 us (2%)
    ppermute x96, waiting for transfers between devices, shifted(): return lax.ppermute(value, axis, pairs)  190 us
    ppermute x96, starting transfers between devices, shifted(): return lax.ppermute(value, axis, pairs)  187 us
    unnamed x2, waiting for transfers between devices  89.7 us
    all_gather x1, blocking collectives, per_device(): lax.all_gather(local_z, 'rep', axis=1, tiled=True)  44.3 us
    all_gather x1, blocking collectives, per_device(): lax.all_gather(vectors, 'rep', axis=1, tiled=True)  44 us
    dot_general x33, matrix products, matern_tile(): lax.dot_general(col_z, row_z, (((0,), (0,)), ((), ())), precision=lax.Pre...  40.8 us
    dot_general x31, matrix products, cols_times(): lax.dot_general(row_v, kernel, (((1,), (1,)), ((), ())), precision=lax.Pr...  26.3 us
    dot_general x33, matrix products, rows_times(): lax.dot(col_v, kernel, precision=lax.Precision.HIGHEST, preferred_element...  19.6 us
  transfers between devices with their start and end apart: 97, of which 65 were waited for; matrix products, arithmetic and copies ran while one was open for 9% of the time, Pallas kernels for 0%

commit v1 on v0

--- a/solution.py
+++ b/solution.py
@@ -43,7 +43,9 @@
 def per_device(points, vectors, lengthscales):
     local_z = points / lengthscales[:, None]
     row_z, row_v = (
-        lax.all_gather(local_z, "rep", axis=1, tiled=True),
+        jnp.concatenate(
+            lax.all_to_all(jnp.stack([local_z] * lax.axis_size("rep")), "rep", 0, 0), axis=1
+        ),
         lax.all_gather(vectors, "rep", axis=1, tiled=True),
     )
     row_sq = jnp.sum(row_z * row_z, axis=0)

time: 668 us -> 633 us (0.948)
  blocking collectives: 88.4 us -> 44.1 us
  starting transfers between devices: 187 us -> 197 us
    all_gather x1 -> x0, blocking collectives: 44.3 us -> none  [per_device(): lax.all_gather(local_z, 'rep', axis=1, tiled=True)]
    all_to_all x0 -> x1, starting transfers between devices: none -> 10.1 us  [per_device(): lax.all_to_all(jnp.stack([local_z] * lax.axis_size('rep')), 'rep', 0, 0)]
  transfers between devices with their start and end apart: 97 -> 98, of which waited for: 65 -> 65; matrix products, arithmetic and copies ran while one was open for 9% -> 9% of each run, Pallas kernels for 0% -> 0%
where the time goes in v1:
time: 633 us; the launch traced here: 630 us
  waiting for transfers between devices  280 us (44%)
  starting transfers between devices  197 us (31%)
  matrix products  86.7 us (14%)
  blocking collectives  44.1 us (7%)
  between operations  13.5 us (2%)
    ppermute x96, waiting for transfers between devices, shifted(): return lax.ppermute(value, axis, pairs)  190 us
    ppermute x96, starting transfers between devices, shifted(): return lax.ppermute(value, axis, pairs)  187 us
    unnamed x2, waiting for transfers between devices  89.5 us
    all_gather x1, blocking collectives, per_device(): lax.all_gather(vectors, 'rep', axis=1, tiled=True)  44.1 us
    dot_general x33, matrix products, matern_tile(): lax.dot_general(col_z, row_z, (((0,), (0,)), ((), ())), precision=lax.Pre...  40.9 us
    dot_general x31, matrix products, cols_times(): lax.dot_general(row_v, kernel, (((1,), (1,)), ((), ())), precision=lax.Pr...  26.3 us
    dot_general x33, matrix products, rows_times(): lax.dot(col_v, kernel, precision=lax.Precision.HIGHEST, preferred_element...  19.6 us
  transfers between devices with their start and end apart: 98, of which 65 were waited for; matrix products, arithmetic and copies ran while one was open for 9% of the time, Pallas kernels for 0%

profile of v1, /device:TPU:2, one launch (start us, length us, event | category | flops | bytes accessed | tf_op | source)
XLA Modules:
  0.0 630.3 jit_solution(4819993507204555412)
XLA Ops:
  8.1 10.1 %all-to-all-start = ((f32[8,16,160]{2,1,0:T(8,128)}), f32[8,16,160]{2,1,0:T(8,128)S(1)}, u32[]{:S(2)}, u32[]{:S(2)}) async-start(f32[8,16,160]{2,1,0:T(8,128)} %stack.2), calls=%async_computation | async-start | bytes 262144 | tf_op jit(solution)/shard_map/all_to_all | solution.py:47
  18.2 44.1 %all-gather = f32[8,160,32]{1,2,0:T(8,128)S(1)} all-gather(f32[1,160,32]{1,2,0:T(8,128)S(1)} %bitcast.51), channel_id=1, replica_groups=mesh['blk'=64,'rep'=8] {'rep'}, dimensions={0}, use_global_device_ids=true | all-gather | bytes 184320 | tf_op jit(solution)/shard_map/all_gather | solution.py:49
  64.7 449.9 %while.17 = (s32[]{:T(128)}, f32[16,160]{1,0:T(8,128)S(1)}, f32[32,160]{1,0:T(8,128)S(1)}, f32[32,160]{1,0:T(8,128)S(1)}, f32[32,1280]{1,0:T(8,128)S(1)}, /*inde...) while((s32[]{:T(128)}, f32[16,160]{1,0:T(8,128)S(1)}, ...), condition=%wide.region_4.0_spmd.clone, body=%wide.region_2.0_spmd.clone.sunk | while | flops 198916960 | bytes 3426791 | solution.py:67
  75.0 3.5 collective-permute-done.1
  85.7 3.2 collective-permute-done
  100.2 3.2 collective-permute-done
  104.7 2.8 collective-permute-done.1
  114.7 3.2 collective-permute-done
  129.2 3.2 collective-permute-done
  143.7 3.2 collective-permute-done
  148.1 2.8 collective-permute-done.1
  158.2 3.2 collective-permute-done
  172.7 3.2 collective-permute-done
  177.1 2.8 collective-permute-done.1
  187.1 3.2 collective-permute-done
  201.6 3.2 collective-permute-done
  216.1 3.2 collective-permute-done
  220.6 2.8 collective-permute-done.1
  230.6 3.2 collective-permute-done
  245.1 3.2 collective-permute-done
  249.5 2.8 collective-permute-done.1
  259.6 3.2 collective-permute-done
  274.1 3.2 collective-permute-done
  288.6 3.2 collective-permute-done
  293.0 2.8 collective-permute-done.1
  303.0 3.2 collective-permute-done
  317.5 3.2 collective-permute-done
  322.0 2.8 collective-permute-done.1
  332.0 3.2 collective-permute-done
  346.5 3.2 collective-permute-done
  361.0 3.2 collective-permute-done
  375.5 3.2 collective-permute-done
  390.0 3.2 collective-permute-done
  394.4 2.8 collective-permute-done.1
  404.5 3.2 collective-permute-done
  418.9 3.2 collective-permute-done
  433.4 3.2 collective-permute-done
  437.9 2.8 collective-permute-done.1
  447.9 3.2 collective-permute-done
  462.4 3.2 collective-permute-done
  466.9 2.8 collective-permute-done.1
  476.9 3.2 collective-permute-done
  491.4 3.2 collective-permute-done
  505.9 3.2 collective-permute-done
  510.3 2.8 collective-permute-done.1
  518.4 5.1 collective-permute-done.4
  528.2 4.2 collective-permute-start.5
  532.4 89.5 %reduce-scatter.4.cloned.1.call-done = f32[160,32]{1,0:T(8,128)} async-done(((f32[1280,32]{1,0:T(8,128)}), f32[160,32]{1,0:T(8,128)}) %reduce-scatter.4.cloned.1.call-update) | async-done | bytes 20496
  (390 shorter events, 332.1 us)
Async XLA Ops:
  8.1 54.5 %all-to-all-start = ((f32[8,16,160]{2,1,0:T(8,128)}), f32[8,16,160]{2,1,0:T(8,128)S(1)}, u32[]{:S(2)}, u32[]{:S(2)}) async-start(f32[8,16,160]{2,1,0:T(8,128)} %stack.2), calls=%async_computation | async-start | bytes 262144 | tf_op jit(solution)/shard_map/all_to_all | solution.py:47
  18.2 603.7 %reduce-scatter.4.cloned.1.call-start = ((), (), s32[]{:S(2)}) async-start(), calls=%async_computation.2 | async-start | bytes 737280
  66.6 12.4 %collective-permute-start.2 = (f32[32,160]{1,0:T(8,128)S(1)}, f32[32,160]{1,0:T(8,128)S(1)}, u32[]{:S(2)}, u32[]{:S(2)}) collective-permute-start(f32[32,160]{1,0:T(8,128)S(1)} %broadcast_select_fusion.2), channel_id=1, source_target_pairs={{0,8},{8,16},{16,24},{24,32},{32,40},{40,48},{48,56},{56,64},{64,7... | collective-permute-start | bytes 61448 | tf_op jit(solution)/shard_map/while/body/eval_jaxpr/ppermute | solution.py:10
  69.3 9.1 %collective-permute-start.1 = (f32[32,160]{1,0:T(8,128)S(1)}, f32[32,160]{1,0:T(8,128)S(1)}, u32[]{:S(2)}, u32[]{:S(2)}) collective-permute-start(f32[32,160]{1,0:T(8,128)S(1)} %get-tuple-element.160), channel_id=1, source_target_pairs={{0,8},{8,16},{16,24},{24,32},{32,40},{40,48},{48,56},{56,64},{64,7... | collective-permute-start | bytes 61448 | tf_op jit(solution)/shard_map/while/body/eval_jaxpr/ppermute | solution.py:10
  81.9 11.7 %collective-permute-start.2 = (f32[32,160]{1,0:T(8,128)S(1)}, f32[32,160]{1,0:T(8,128)S(1)}, u32[]{:S(2)}, u32[]{:S(2)}) collective-permute-start(f32[32,160]{1,0:T(8,128)S(1)} %broadcast_select_fusion.2), channel_id=1, source_target_pairs={{0,8},{8,16},{16,24},{24,32},{32,40},{40,48},{48,56},{56,64},{64,7... | collective-permute-start | bytes 61448 | tf_op jit(solution)/shard_map/while/body/eval_jaxpr/ppermute | solution.py:10
  83.8 9.1 %collective-permute-start.1 = (f32[32,160]{1,0:T(8,128)S(1)}, f32[32,160]{1,0:T(8,128)S(1)}, u32[]{:S(2)}, u32[]{:S(2)}) collective-permute-start(f32[32,160]{1,0:T(8,128)S(1)} %get-tuple-element.160), channel_id=1, source_target_pairs={{0,8},{8,16},{16,24},{24,32},{32,40},{40,48},{48,56},{56,64},{64,7... | collective-permute-start | bytes 61448 | tf_op jit(solution)/shard_map/while/body/eval_jaxpr/ppermute | solution.py:10
  96.4 11.7 %collective-permute-start.2 = (f32[32,160]{1,0:T(8,128)S(1)}, f32[32,160]{1,0:T(8,128)S(1)}, u32[]{:S(2)}, u32[]{:S(2)}) collective-permute-start(f32[32,160]{1,0:T(8,128)S(1)} %broadcast_select_fusion.2), channel_id=1, source_target_pairs={{0,8},{8,16},{16,24},{24,32},{32,40},{40,48},{48,56},{56,64},{64,7... | collective-permute-start | bytes 61448 | tf_op jit(solution)/shard_map/while/body/eval_jaxpr/ppermute | solution.py:10
  110.8 11.7 %collective-permute-start.2 = (f32[32,160]{1,0:T(8,128)S(1)}, f32[32,160]{1,0:T(8,128)S(1)}, u32[]{:S(2)}, u32[]{:S(2)}) collective-permute-start(f32[32,160]{1,0:T(8,128)S(1)} %broadcast_select_fusion.2), channel_id=1, source_target_pairs={{0,8},{8,16},{16,24},{24,32},{32,40},{40,48},{48,56},{56,64},{64,7... | collective-permute-start | bytes 61448 | tf_op jit(solution)/shard_map/while/body/eval_jaxpr/ppermute | solution.py:10
  112.8 9.1 %collective-permute-start.1 = (f32[32,160]{1,0:T(8,128)S(1)}, f32[32,160]{1,0:T(8,128)S(1)}, u32[]{:S(2)}, u32[]{:S(2)}) collective-permute-start(f32[32,160]{1,0:T(8,128)S(1)} %get-tuple-element.160), channel_id=1, source_target_pairs={{0,8},{8,16},{16,24},{24,32},{32,40},{40,48},{48,56},{56,64},{64,7... | collective-permute-start | bytes 61448 | tf_op jit(solution)/shard_map/while/body/eval_jaxpr/ppermute | solution.py:10
  125.3 11.7 %collective-permute-start.2 = (f32[32,160]{1,0:T(8,128)S(1)}, f32[32,160]{1,0:T(8,128)S(1)}, u32[]{:S(2)}, u32[]{:S(2)}) collective-permute-start(f32[32,160]{1,0:T(8,128)S(1)} %broadcast_select_fusion.2), channel_id=1, source_target_pairs={{0,8},{8,16},{16,24},{24,32},{32,40},{40,48},{48,56},{56,64},{64,7... | collective-permute-start | bytes 61448 | tf_op jit(solution)/shard_map/while/body/eval_jaxpr/ppermute | solution.py:10
  127.3 9.1 %collective-permute-start.1 = (f32[32,160]{1,0:T(8,128)S(1)}, f32[32,160]{1,0:T(8,128)S(1)}, u32[]{:S(2)}, u32[]{:S(2)}) collective-permute-start(f32[32,160]{1,0:T(8,128)S(1)} %get-tuple-element.160), channel_id=1, source_target_pairs={{0,8},{8,16},{16,24},{24,32},{32,40},{40,48},{48,56},{56,64},{64,7... | collective-permute-start | bytes 61448 | tf_op jit(solution)/shard_map/while/body/eval_jaxpr/ppermute | solution.py:10
  139.8 11.7 %collective-permute-start.2 = (f32[32,160]{1,0:T(8,128)S(1)}, f32[32,160]{1,0:T(8,128)S(1)}, u32[]{:S(2)}, u32[]{:S(2)}) collective-permute-start(f32[32,160]{1,0:T(8,128)S(1)} %broadcast_select_fusion.2), channel_id=1, source_target_pairs={{0,8},{8,16},{16,24},{24,32},{32,40},{40,48},{48,56},{56,64},{64,7... | collective-permute-start | bytes 61448 | tf_op jit(solution)/shard_map/while/body/eval_jaxpr/ppermute | solution.py:10
  154.3 11.7 %collective-permute-start.2 = (f32[32,160]{1,0:T(8,128)S(1)}, f32[32,160]{1,0:T(8,128)S(1)}, u32[]{:S(2)}, u32[]{:S(2)}) collective-permute-start(f32[32,160]{1,0:T(8,128)S(1)} %broadcast_select_fusion.2), channel_id=1, source_target_pairs={{0,8},{8,16},{16,24},{24,32},{32,40},{40,48},{48,56},{56,64},{64,7... | collective-permute-start | bytes 61448 | tf_op jit(solution)/shard_map/while/body/eval_jaxpr/ppermute | solution.py:10
  168.8 11.7 %collective-permute-start.2 = (f32[32,160]{1,0:T(8,128)S(1)}, f32[32,160]{1,0:T(8,128)S(1)}, u32[]{:S(2)}, u32[]{:S(2)}) collective-permute-start(f32[32,160]{1,0:T(8,128)S(1)} %broadcast_select_fusion.2), channel_id=1, source_target_pairs={{0,8},{8,16},{16,24},{24,32},{32,40},{40,48},{48,56},{56,64},{64,7... | collective-permute-start | bytes 61448 | tf_op jit(solution)/shard_map/while/body/eval_jaxpr/ppermute | solution.py:10
  170.7 9.1 %collective-permute-start.1 = (f32[32,160]{1,0:T(8,128)S(1)}, f32[32,160]{1,0:T(8,128)S(1)}, u32[]{:S(2)}, u32[]{:S(2)}) collective-permute-start(f32[32,160]{1,0:T(8,128)S(1)} %get-tuple-element.160), channel_id=1, source_target_pairs={{0,8},{8,16},{16,24},{24,32},{32,40},{40,48},{48,56},{56,64},{64,7... | collective-permute-start | bytes 61448 | tf_op jit(solution)/shard_map/while/body/eval_jaxpr/ppermute | solution.py:10
  183.3 11.7 %collective-permute-start.2 = (f32[32,160]{1,0:T(8,128)S(1)}, f32[32,160]{1,0:T(8,128)S(1)}, u32[]{:S(2)}, u32[]{:S(2)}) collective-permute-start(f32[32,160]{1,0:T(8,128)S(1)} %broadcast_select_fusion.2), channel_id=1, source_target_pairs={{0,8},{8,16},{16,24},{24,32},{32,40},{40,48},{48,56},{56,64},{64,7... | collective-permute-start | bytes 61448 | tf_op jit(solution)/shard_map/while/body/eval_jaxpr/ppermute | solution.py:10
  185.2 9.1 %collective-permute-start.1 = (f32[32,160]{1,0:T(8,128)S(1)}, f32[32,160]{1,0:T(8,128)S(1)}, u32[]{:S(2)}, u32[]{:S(2)}) collective-permute-start(f32[32,160]{1,0:T(8,128)S(1)} %get-tuple-element.160), channel_id=1, source_target_pairs={{0,8},{8,16},{16,24},{24,32},{32,40},{40,48},{48,56},{56,64},{64,7... | collective-permute-start | bytes 61448 | tf_op jit(solution)/shard_map/while/body/eval_jaxpr/ppermute | solution.py:10
  197.8 11.7 %collective-permute-start.2 = (f32[32,160]{1,0:T(8,128)S(1)}, f32[32,160]{1,0:T(8,128)S(1)}, u32[]{:S(2)}, u32[]{:S(2)}) collective-permute-start(f32[32,160]{1,0:T(8,128)S(1)} %broadcast_select_fusion.2), channel_id=1, source_target_pairs={{0,8},{8,16},{16,24},{24,32},{32,40},{40,48},{48,56},{56,64},{64,7... | collective-permute-start | bytes 61448 | tf_op jit(solution)/shard_map/while/body/eval_jaxpr/ppermute | solution.py:10
  199.7 9.1 %collective-permute-start.1 = (f32[32,160]{1,0:T(8,128)S(1)}, f32[32,160]{1,0:T(8,128)S(1)}, u32[]{:S(2)}, u32[]{:S(2)}) collective-permute-start(f32[32,160]{1,0:T(8,128)S(1)} %get-tuple-element.160), channel_id=1, source_target_pairs={{0,8},{8,16},{16,24},{24,32},{32,40},{40,48},{48,56},{56,64},{64,7... | collective-permute-start | bytes 61448 | tf_op jit(solution)/shard_map/while/body/eval_jaxpr/ppermute | solution.py:10
  212.3 11.7 %collective-permute-start.2 = (f32[32,160]{1,0:T(8,128)S(1)}, f32[32,160]{1,0:T(8,128)S(1)}, u32[]{:S(2)}, u32[]{:S(2)}) collective-permute-start(f32[32,160]{1,0:T(8,128)S(1)} %broadcast_select_fusion.2), channel_id=1, source_target_pairs={{0,8},{8,16},{16,24},{24,32},{32,40},{40,48},{48,56},{56,64},{64,7... | collective-permute-start | bytes 61448 | tf_op jit(solution)/shard_map/while/body/eval_jaxpr/ppermute | solution.py:10
  214.2 9.1 %collective-permute-start.1 = (f32[32,160]{1,0:T(8,128)S(1)}, f32[32,160]{1,0:T(8,128)S(1)}, u32[]{:S(2)}, u32[]{:S(2)}) collective-permute-start(f32[32,160]{1,0:T(8,128)S(1)} %get-tuple-element.160), channel_id=1, source_target_pairs={{0,8},{8,16},{16,24},{24,32},{32,40},{40,48},{48,56},{56,64},{64,7... | collective-permute-start | bytes 61448 | tf_op jit(solution)/shard_map/while/body/eval_jaxpr/ppermute | solution.py:10
  226.7 11.7 %collective-permute-start.2 = (f32[32,160]{1,0:T(8,128)S(1)}, f32[32,160]{1,0:T(8,128)S(1)}, u32[]{:S(2)}, u32[]{:S(2)}) collective-permute-start(f32[32,160]{1,0:T(8,128)S(1)} %broadcast_select_fusion.2), channel_id=1, source_target_pairs={{0,8},{8,16},{16,24},{24,32},{32,40},{40,48},{48,56},{56,64},{64,7... | collective-permute-start | bytes 61448 | tf_op jit(solution)/shard_map/while/body/eval_jaxpr/ppermute | solution.py:10
  228.7 9.1 %collective-permute-start.1 = (f32[32,160]{1,0:T(8,128)S(1)}, f32[32,160]{1,0:T(8,128)S(1)}, u32[]{:S(2)}, u32[]{:S(2)}) collective-permute-start(f32[32,160]{1,0:T(8,128)S(1)} %get-tuple-element.160), channel_id=1, source_target_pairs={{0,8},{8,16},{16,24},{24,32},{32,40},{40,48},{48,56},{56,64},{64,7... | collective-permute-start | bytes 61448 | tf_op jit(solution)/shard_map/while/body/eval_jaxpr/ppermute | solution.py:10
  241.2 11.7 %collective-permute-start.2 = (f32[32,160]{1,0:T(8,128)S(1)}, f32[32,160]{1,0:T(8,128)S(1)}, u32[]{:S(2)}, u32[]{:S(2)}) collective-permute-start(f32[32,160]{1,0:T(8,128)S(1)} %broadcast_select_fusion.2), channel_id=1, source_target_pairs={{0,8},{8,16},{16,24},{24,32},{32,40},{40,48},{48,56},{56,64},{64,7... | collective-permute-start | bytes 61448 | tf_op jit(solution)/shard_map/while/body/eval_jaxpr/ppermute | solution.py:10
  243.2 9.1 %collective-permute-start.1 = (f32[32,160]{1,0:T(8,128)S(1)}, f32[32,160]{1,0:T(8,128)S(1)}, u32[]{:S(2)}, u32[]{:S(2)}) collective-permute-start(f32[32,160]{1,0:T(8,128)S(1)} %get-tuple-element.160), channel_id=1, source_target_pairs={{0,8},{8,16},{16,24},{24,32},{32,40},{40,48},{48,56},{56,64},{64,7... | collective-permute-start | bytes 61448 | tf_op jit(solution)/shard_map/while/body/eval_jaxpr/ppermute | solution.py:10
  255.7 11.7 %collective-permute-start.2 = (f32[32,160]{1,0:T(8,128)S(1)}, f32[32,160]{1,0:T(8,128)S(1)}, u32[]{:S(2)}, u32[]{:S(2)}) collective-permute-start(f32[32,160]{1,0:T(8,128)S(1)} %broadcast_select_fusion.2), channel_id=1, source_target_pairs={{0,8},{8,16},{16,24},{24,32},{32,40},{40,48},{48,56},{56,64},{64,7... | collective-permute-start | bytes 61448 | tf_op jit(solution)/shard_map/while/body/eval_jaxpr/ppermute | solution.py:10
  257.7 9.1 %collective-permute-start.1 = (f32[32,160]{1,0:T(8,128)S(1)}, f32[32,160]{1,0:T(8,128)S(1)}, u32[]{:S(2)}, u32[]{:S(2)}) collective-permute-start(f32[32,160]{1,0:T(8,128)S(1)} %get-tuple-element.160), channel_id=1, source_target_pairs={{0,8},{8,16},{16,24},{24,32},{32,40},{40,48},{48,56},{56,64},{64,7... | collective-permute-start | bytes 61448 | tf_op jit(solution)/shard_map/while/body/eval_jaxpr/ppermute | solution.py:10
  270.2 11.7 %collective-permute-start.2 = (f32[32,160]{1,0:T(8,128)S(1)}, f32[32,160]{1,0:T(8,128)S(1)}, u32[]{:S(2)}, u32[]{:S(2)}) collective-permute-start(f32[32,160]{1,0:T(8,128)S(1)} %broadcast_select_fusion.2), channel_id=1, source_target_pairs={{0,8},{8,16},{16,24},{24,32},{32,40},{40,48},{48,56},{56,64},{64,7... | collective-permute-start | bytes 61448 | tf_op jit(solution)/shard_map/while/body/eval_jaxpr/ppermute | solution.py:10
  284.7 11.7 %collective-permute-start.2 = (f32[32,160]{1,0:T(8,128)S(1)}, f32[32,160]{1,0:T(8,128)S(1)}, u32[]{:S(2)}, u32[]{:S(2)}) collective-permute-start(f32[32,160]{1,0:T(8,128)S(1)} %broadcast_select_fusion.2), channel_id=1, source_target_pairs={{0,8},{8,16},{16,24},{24,32},{32,40},{40,48},{48,56},{56,64},{64,7... | collective-permute-start | bytes 61448 | tf_op jit(solution)/shard_map/while/body/eval_jaxpr/ppermute | solution.py:10
  286.6 9.1 %collective-permute-start.1 = (f32[32,160]{1,0:T(8,128)S(1)}, f32[32,160]{1,0:T(8,128)S(1)}, u32[]{:S(2)}, u32[]{:S(2)}) collective-permute-start(f32[32,160]{1,0:T(8,128)S(1)} %get-tuple-element.160), channel_id=1, source_target_pairs={{0,8},{8,16},{16,24},{24,32},{32,40},{40,48},{48,56},{56,64},{64,7... | collective-permute-start | bytes 61448 | tf_op jit(solution)/shard_map/while/body/eval_jaxpr/ppermute | solution.py:10
  299.2 11.7 %collective-permute-start.2 = (f32[32,160]{1,0:T(8,128)S(1)}, f32[32,160]{1,0:T(8,128)S(1)}, u32[]{:S(2)}, u32[]{:S(2)}) collective-permute-start(f32[32,160]{1,0:T(8,128)S(1)} %broadcast_select_fusion.2), channel_id=1, source_target_pairs={{0,8},{8,16},{16,24},{24,32},{32,40},{40,48},{48,56},{56,64},{64,7... | collective-permute-start | bytes 61448 | tf_op jit(solution)/shard_map/while/body/eval_jaxpr/ppermute | solution.py:10
  301.1 9.1 %collective-permute-start.1 = (f32[32,160]{1,0:T(8,128)S(1)}, f32[32,160]{1,0:T(8,128)S(1)}, u32[]{:S(2)}, u32[]{:S(2)}) collective-permute-start(f32[32,160]{1,0:T(8,128)S(1)} %get-tuple-element.160), channel_id=1, source_target_pairs={{0,8},{8,16},{16,24},{24,32},{32,40},{40,48},{48,56},{56,64},{64,7... | collective-permute-start | bytes 61448 | tf_op jit(solution)/shard_map/while/body/eval_jaxpr/ppermute | solution.py:10
  313.7 11.7 %collective-permute-start.2 = (f32[32,160]{1,0:T(8,128)S(1)}, f32[32,160]{1,0:T(8,128)S(1)}, u32[]{:S(2)}, u32[]{:S(2)}) collective-permute-start(f32[32,160]{1,0:T(8,128)S(1)} %broadcast_select_fusion.2), channel_id=1, source_target_pairs={{0,8},{8,16},{16,24},{24,32},{32,40},{40,48},{48,56},{56,64},{64,7... | collective-permute-start | bytes 61448 | tf_op jit(solution)/shard_map/while/body/eval_jaxpr/ppermute | solution.py:10
  328.2 11.7 %collective-permute-start.2 = (f32[32,160]{1,0:T(8,128)S(1)}, f32[32,160]{1,0:T(8,128)S(1)}, u32[]{:S(2)}, u32[]{:S(2)}) collective-permute-start(f32[32,160]{1,0:T(8,128)S(1)} %broadcast_select_fusion.2), channel_id=1, source_target_pairs={{0,8},{8,16},{16,24},{24,32},{32,40},{40,48},{48,56},{56,64},{64,7... | collective-permute-start | bytes 61448 | tf_op jit(solution)/shard_map/while/body/eval_jaxpr/ppermute | solution.py:10
  342.6 11.7 %collective-permute-start.2 = (f32[32,160]{1,0:T(8,128)S(1)}, f32[32,160]{1,0:T(8,128)S(1)}, u32[]{:S(2)}, u32[]{:S(2)}) collective-permute-start(f32[32,160]{1,0:T(8,128)S(1)} %broadcast_select_fusion.2), channel_id=1, source_target_pairs={{0,8},{8,16},{16,24},{24,32},{32,40},{40,48},{48,56},{56,64},{64,7... | collective-permute-start | bytes 61448 | tf_op jit(solution)/shard_map/while/body/eval_jaxpr/ppermute | solution.py:10
  357.1 11.7 %collective-permute-start.2 = (f32[32,160]{1,0:T(8,128)S(1)}, f32[32,160]{1,0:T(8,128)S(1)}, u32[]{:S(2)}, u32[]{:S(2)}) collective-permute-start(f32[32,160]{1,0:T(8,128)S(1)} %broadcast_select_fusion.2), channel_id=1, source_target_pairs={{0,8},{8,16},{16,24},{24,32},{32,40},{40,48},{48,56},{56,64},{64,7... | collective-permute-start | bytes 61448 | tf_op jit(solution)/shard_map/while/body/eval_jaxpr/ppermute | solution.py:10
  371.6 11.7 %collective-permute-start.2 = (f32[32,160]{1,0:T(8,128)S(1)}, f32[32,160]{1,0:T(8,128)S(1)}, u32[]{:S(2)}, u32[]{:S(2)}) collective-permute-start(f32[32,160]{1,0:T(8,128)S(1)} %broadcast_select_fusion.2), channel_id=1, source_target_pairs={{0,8},{8,16},{16,24},{24,32},{32,40},{40,48},{48,56},{56,64},{64,7... | collective-permute-start | bytes 61448 | tf_op jit(solution)/shard_map/while/body/eval_jaxpr/ppermute | solution.py:10
  386.1 11.7 %collective-permute-start.2 = (f32[32,160]{1,0:T(8,128)S(1)}, f32[32,160]{1,0:T(8,128)S(1)}, u32[]{:S(2)}, u32[]{:S(2)}) collective-permute-start(f32[32,160]{1,0:T(8,128)S(1)} %broadcast_select_fusion.2), channel_id=1, source_target_pairs={{0,8},{8,16},{16,24},{24,32},{32,40},{40,48},{48,56},{56,64},{64,7... | collective-permute-start | bytes 61448 | tf_op jit(solution)/shard_map/while/body/eval_jaxpr/ppermute | solution.py:10
  400.6 11.7 %collective-permute-start.2 = (f32[32,160]{1,0:T(8,128)S(1)}, f32[32,160]{1,0:T(8,128)S(1)}, u32[]{:S(2)}, u32[]{:S(2)}) collective-permute-start(f32[32,160]{1,0:T(8,128)S(1)} %broadcast_select_fusion.2), channel_id=1, source_target_pairs={{0,8},{8,16},{16,24},{24,32},{32,40},{40,48},{48,56},{56,64},{64,7... | collective-permute-start | bytes 61448 | tf_op jit(solution)/shard_map/while/body/eval_jaxpr/ppermute | solution.py:10
  415.1 11.7 %collective-permute-start.2 = (f32[32,160]{1,0:T(8,128)S(1)}, f32[32,160]{1,0:T(8,128)S(1)}, u32[]{:S(2)}, u32[]{:S(2)}) collective-permute-start(f32[32,160]{1,0:T(8,128)S(1)} %broadcast_select_fusion.2), channel_id=1, source_target_pairs={{0,8},{8,16},{16,24},{24,32},{32,40},{40,48},{48,56},{56,64},{64,7... | collective-permute-start | bytes 61448 | tf_op jit(solution)/shard_map/while/body/eval_jaxpr/ppermute | solution.py:10
  429.6 11.7 %collective-permute-start.2 = (f32[32,160]{1,0:T(8,128)S(1)}, f32[32,160]{1,0:T(8,128)S(1)}, u32[]{:S(2)}, u32[]{:S(2)}) collective-permute-start(f32[32,160]{1,0:T(8,128)S(1)} %broadcast_select_fusion.2), channel_id=1, source_target_pairs={{0,8},{8,16},{16,24},{24,32},{32,40},{40,48},{48,56},{56,64},{64,7... | collective-permute-start | bytes 61448 | tf_op jit(solution)/shard_map/while/body/eval_jaxpr/ppermute | solution.py:10
  444.1 11.7 %collective-permute-start.2 = (f32[32,160]{1,0:T(8,128)S(1)}, f32[32,160]{1,0:T(8,128)S(1)}, u32[]{:S(2)}, u32[]{:S(2)}) collective-permute-start(f32[32,160]{1,0:T(8,128)S(1)} %broadcast_select_fusion.2), channel_id=1, source_target_pairs={{0,8},{8,16},{16,24},{24,32},{32,40},{40,48},{48,56},{56,64},{64,7... | collective-permute-start | bytes 61448 | tf_op jit(solution)/shard_map/while/body/eval_jaxpr/ppermute | solution.py:10
  458.6 11.7 %collective-permute-start.2 = (f32[32,160]{1,0:T(8,128)S(1)}, f32[32,160]{1,0:T(8,128)S(1)}, u32[]{:S(2)}, u32[]{:S(2)}) collective-permute-start(f32[32,160]{1,0:T(8,128)S(1)} %broadcast_select_fusion.2), channel_id=1, source_target_pairs={{0,8},{8,16},{16,24},{24,32},{32,40},{40,48},{48,56},{56,64},{64,7... | collective-permute-start | bytes 61448 | tf_op jit(solution)/shard_map/while/body/eval_jaxpr/ppermute | solution.py:10
  473.0 11.7 %collective-permute-start.2 = (f32[32,160]{1,0:T(8,128)S(1)}, f32[32,160]{1,0:T(8,128)S(1)}, u32[]{:S(2)}, u32[]{:S(2)}) collective-permute-start(f32[32,160]{1,0:T(8,128)S(1)} %broadcast_select_fusion.2), channel_id=1, source_target_pairs={{0,8},{8,16},{16,24},{24,32},{32,40},{40,48},{48,56},{56,64},{64,7... | collective-permute-start | bytes 61448 | tf_op jit(solution)/shard_map/while/body/eval_jaxpr/ppermute | solution.py:10
  487.5 11.7 %collective-permute-start.2 = (f32[32,160]{1,0:T(8,128)S(1)}, f32[32,160]{1,0:T(8,128)S(1)}, u32[]{:S(2)}, u32[]{:S(2)}) collective-permute-start(f32[32,160]{1,0:T(8,128)S(1)} %broadcast_select_fusion.2), channel_id=1, source_target_pairs={{0,8},{8,16},{16,24},{24,32},{32,40},{40,48},{48,56},{56,64},{64,7... | collective-permute-start | bytes 61448 | tf_op jit(solution)/shard_map/while/body/eval_jaxpr/ppermute | solution.py:10
  502.0 11.7 %collective-permute-start.2 = (f32[32,160]{1,0:T(8,128)S(1)}, f32[32,160]{1,0:T(8,128)S(1)}, u32[]{:S(2)}, u32[]{:S(2)}) collective-permute-start(f32[32,160]{1,0:T(8,128)S(1)} %broadcast_select_fusion.2), channel_id=1, source_target_pairs={{0,8},{8,16},{16,24},{24,32},{32,40},{40,48},{48,56},{56,64},{64,7... | collective-permute-start | bytes 61448 | tf_op jit(solution)/shard_map/while/body/eval_jaxpr/ppermute | solution.py:10
  516.5 9.4 %collective-permute-start.3 = (f32[32,160]{1,0:T(8,128)S(1)}, f32[32,160]{1,0:T(8,128)S(1)}, u32[]{:S(2)}, u32[]{:S(2)}) collective-permute-start(f32[32,160]{1,0:T(8,128)S(1)} %get-tuple-element.51), channel_id=1, source_target_pairs={{0,8},{8,16},{16,24},{24,32},{32,40},{40,48},{48,56},{56,64},{64,7... | collective-permute-start | bytes 61448 | tf_op jit(solution)/shard_map/ppermute | solution.py:10
  528.2 94.6 %collective-permute-start.5 = (f32[32,160]{1,0:T(8,128)S(1)}, f32[32,160]{1,0:T(8,128)S(1)}, u32[]{:S(2)}, u32[]{:S(2)}) collective-permute-start(f32[32,160]{1,0:T(8,128)S(1)} %get-tuple-element.53), channel_id=1, source_target_pairs={{0,264},{8,272},{16,280},{24,288},{32,296},{40,304},{48,312},{56,3... | collective-permute-start | bytes 61448 | tf_op jit(solution)/shard_map/ppermute | solution.py:10
  (52 other events, 453.0 us)
Sparse Core Ops, SparseCore 0:
  528.3 93.5 reduce-scatter.3
